TPU v7x, 512 devices: a whole 4x4x16 slice. The times are simulated.
512 devices in a mesh: grp: 16 (over z), dev: 32 (over y, x, core).
Axes of the slice: x: 4, y: 4, z: 16, core: 2. Of those that a mesh axis runs over, the one named last changes fastest.
Arguments:
- particles: bfloat16 [8192, 2, 6144], P(('grp', 'dev')), may hold values from -24 to 24
- defocus_bin: int32 [8192], P(('grp', 'dev')), may hold values from 0 to 15
- candidates: int32 [8192, 8], P(('grp', 'dev')), may hold values from 0 to 63, as said below
- projections: bfloat16 [64, 2, 6144], P('dev'), may hold values from -1 to 1
- ctf_table: bfloat16 [16, 6144], replicated, may hold values from -1 to 1
- inv_noise: float32 [6144], replicated, may hold values from 0.25 to 4
- line_slab: int32 [64, 48], P('dev'), may hold values from 0 to 15, as said below
- slab_owner: int32 [16], replicated, may hold values from 0 to 15, each once
Outputs:
- slab_data: float32 [16, 64, 2, 6, 128], P('grp', 'dev')
- slab_weight: float32 [16, 64, 6, 128], P('grp', 'dev')
Inputs may be any that keep to these rules, and one draw needn't show every extreme that they name: `candidates`: each particle lists 8 different projections. `line_slab`: no slab holds more than 6 lines of one projection, and for every projection one slab holds exactly 6 of them. `slab_owner`: each group owns exactly one slab.
All inputs are finite; a program needn't handle non-finite values.
Results may differ from a plain program's by a relative error of at most 0.02.
Values may be sent and summed in bfloat16 or wider, within the bound.
A program may use at most 64 MiB of HBM per device.

v0:
```python
import math
import jax
import jax.numpy as jnp
from jax import lax
from jax.sharding import PartitionSpec as P

LINE_LEN = 128
PIXELS = 6144
SHIFTS = 9
two_pi = 2.0 * math.pi
exact = lax.Precision.HIGHEST
contract_rows = (((0,), (0,)), ((), ()))
contract_last = (((1,), (1,)), ((), ()))


def phase_tables():
    pixel_index = jnp.arange(PIXELS, dtype=jnp.int32)
    line_pos = (pixel_index // LINE_LEN).astype(jnp.float32)
    column = pixel_index % LINE_LEN
    frequency = jnp.where(column < LINE_LEN // 2, column, column - LINE_LEN).astype(jnp.float32)
    shift_index = jnp.arange(SHIFTS, dtype=jnp.int32)
    move_x = (shift_index // 3 - 1).astype(jnp.float32)
    move_y = (shift_index % 3 - 1).astype(jnp.float32)
    angles = (move_x[:, None] * line_pos[None, :] + move_y[:, None] * frequency[None, :]) * (
        two_pi / LINE_LEN
    )
    return (jnp.cos(angles), jnp.sin(angles))


def slot_tables(line_slab, slab_owner, groups):
    group_ids = jnp.arange(groups, dtype=jnp.int32)
    slab_hit = line_slab[:, :, None] == group_ids[None, None, :]
    owner_line = jnp.sum(jnp.where(slab_hit, slab_owner[None, None, :], 0), axis=2)
    line_ids = jnp.arange(line_slab.shape[1], dtype=jnp.int32)
    earlier = line_ids[None, :] < line_ids[:, None]
    same_owner = owner_line[:, :, None] == owner_line[:, None, :]
    line_rank = jnp.sum(jnp.logical_and(same_owner, earlier[None]), axis=2)
    return (owner_line, line_rank)


def route_lines(values, owner_line, line_rank, groups, capacity):
    group_ids = jnp.arange(groups, dtype=jnp.int32)
    slot_ids = jnp.arange(capacity, dtype=jnp.int32)
    selector = jnp.logical_and(
        owner_line[:, None, None, :] == group_ids[None, :, None, None],
        line_rank[:, None, None, :] == slot_ids[None, None, :, None],
    ).astype(jnp.float32)
    packed = jnp.einsum("jocl,jxlp->ojxcp", selector, values, precision=exact)
    return lax.psum_scatter(
        packed.astype(jnp.bfloat16), "grp", scatter_dimension=0, tiled=True
    ).astype(jnp.float32)[0]


def body(
    particles, defocus_bin, candidates, projections, ctf_table, inv_noise, line_slab, slab_owner
):
    part_dev = particles.shape[0]
    pixels = particles.shape[2]
    proj_dev = projections.shape[0]
    groups = lax.axis_size("grp")
    members = lax.axis_size("dev")
    proj_all = proj_dev * members
    line_count = line_slab.shape[1]
    line_len = pixels // line_count
    capacity = 2 * line_count // groups
    cosines, sine_table = phase_tables()
    table_values = ctf_table.astype(jnp.float32)
    ctf_square = table_values * table_values
    noisy_square = ctf_square * inv_noise[None, :]
    onehot = (
        defocus_bin[:, None] == jnp.arange(ctf_table.shape[0], dtype=jnp.int32)[None, :]
    ).astype(jnp.float32)
    ctf_rows = jnp.dot(onehot, table_values, precision=exact)
    weighted = (
        ((inv_noise[None, :] * ctf_rows)[:, None, :] * particles)
        .astype(jnp.bfloat16)
        .reshape(part_dev, 2 * pixels)
    )
    ctf_image = (
        (ctf_rows[:, None, :] * particles).astype(jnp.bfloat16).reshape(part_dev, 2 * pixels)
    )
    values = lax.all_gather(projections, "dev", axis=0, tiled=True).astype(jnp.float32)
    pix_power = values[:, 0] * values[:, 0] + values[:, 1] * values[:, 1]
    bin_power = lax.dot_general(noisy_square, pix_power, contract_last, precision=exact)
    quad_term = jnp.dot(onehot, bin_power, precision=exact)

    def one_shift(tables):
        cos_row, sin_row = tables
        real_part = values[:, 0] * cos_row[None, :] - values[:, 1] * sin_row[None, :]
        imag_part = values[:, 0] * sin_row[None, :] + values[:, 1] * cos_row[None, :]
        rotated = jnp.concatenate([real_part, imag_part], axis=1).astype(jnp.bfloat16)
        return lax.dot_general(weighted, rotated, contract_last, preferred_element_type=jnp.float32)

    scored = lax.map(one_shift, (cosines, sine_table))
    scores = jnp.transpose(scored, (1, 0, 2)) - 0.5 * quad_term[:, None, :]
    proj_ids = jnp.arange(proj_all, dtype=jnp.int32)
    listed = jnp.any(candidates[:, :, None] == proj_ids[None, None, :], axis=1)
    masked = jnp.where(listed[:, None, :], scores, -jnp.inf)
    row_peak = jnp.max(masked, axis=(1, 2), keepdims=True)
    exp_terms = jnp.exp(masked - row_peak)
    posterior = exp_terms / jnp.sum(exp_terms, axis=(1, 2), keepdims=True)
    by_shift = jnp.transpose(posterior.astype(jnp.bfloat16), (1, 0, 2))

    def add_shift(running, inputs):
        weights_now, cos_row, sin_row = inputs
        summed = lax.dot_general(
            weights_now, ctf_image, contract_rows, preferred_element_type=jnp.float32
        )
        real_sum = summed[:, :pixels]
        imag_sum = summed[:, pixels:]
        turned = jnp.stack(
            [
                real_sum * cos_row[None, :] + imag_sum * sin_row[None, :],
                imag_sum * cos_row[None, :] - real_sum * sin_row[None, :],
            ],
            axis=1,
        )
        return (running + turned, None)

    start_sum = jnp.zeros((proj_dev * lax.axis_size("dev"), 2, pixels), jnp.float32)
    result, _ = lax.scan(add_shift, start_sum, (by_shift, cosines, sine_table))
    data_part = lax.psum_scatter(
        result.astype(jnp.bfloat16), "dev", scatter_dimension=0, tiled=True
    ).astype(jnp.float32)
    proj_share = jnp.sum(posterior, axis=1)
    weight_scale = proj_all / (part_dev * groups * members)
    owner_line, line_rank = slot_tables(line_slab, slab_owner, groups)
    data_lines = data_part.reshape(proj_dev, 2, line_count, line_len)
    ctf_rows_sq = ctf_rows * ctf_rows
    weight_part = (
        lax.psum_scatter(
            lax.dot_general(
                proj_share,
                ctf_rows_sq,
                contract_rows,
                precision=exact,
                preferred_element_type=jnp.float32,
            ).astype(jnp.bfloat16),
            "dev",
            scatter_dimension=0,
            tiled=True,
        ).astype(jnp.float32)
        * weight_scale
    )
    stacked = jnp.concatenate(
        [data_lines, weight_part.reshape(proj_dev, 1, line_count, line_len)], axis=1
    )
    routed = route_lines(stacked, owner_line, line_rank, groups, capacity)
    return (routed[None, :, :2], routed[None, :, 2])


def solution(mesh):
    return jax.shard_map(
        body,
        mesh=mesh,
        in_specs=(
            P(("grp", "dev"), None, None),
            P(("grp", "dev")),
            P(("grp", "dev"), None),
            P("dev", None, None),
            P(),
            P(),
            P("dev", None),
            P(),
        ),
        out_specs=(P("grp", "dev", None, None, None), P("grp", "dev", None, None)),
        check_vma=False,
    )
```

profile of v0, /device:TPU:2, one launch (start us, length us, event | category | flops | bytes accessed | tf_op | source)
XLA Modules:
  0.0 495.3 jit_solution(7120821625978491027)
XLA Ops:
  9.2 1.8 fusion.25
  12.2 2.4 fusion.30
  14.6 59.3 %all-gather.2.cloned.1.call-done = bf16[64,2,6144]{2,1,0:T(2,128)(2,1)} async-done(((bf16[2,2,6144]{2,1,0:T(2,128)(2,1)}), bf16[64,2,6144]{2,1,0:T(2,128)(2,1)}) %all-gather.2.cloned.1.call-update) | async-done | bytes 1572880 | tf_op jit(solution)/shard_map/all_gather | solution.py:82
  73.8 3.2 convert_element_type.95
  77.0 3.0 fusion.19
  80.0 59.7 %while.21 = (s32[]{:T(128)}, f32[9,16,64]{2,1,0:T(8,128)}, f32[64,2,6144]{2,1,0:T(2,128)S(1)}, f32[9,6144]{1,0:T(8,128)}, f32[9,6144]{1,0:T(8,128)}, /*index=5*/bf16[16,12288]{1,0:T(8,128)(2,1)}, s32[]{:T(128)}) while((s32[]{:T(128)}, f32[9,16,64]{2,1,0:T(8,128)}, f32[64,2,6144]{2,1,0:T(2,128)S(1)}, f32[9,6144]{1,0:T(8,128)}, ...), condition=%wide.region_2.3_spmd, body=%wide.region_1.2_spmd.sunk | while | flops 31457280 | bytes 17850988 | solution.py:94
  81.1 1.8 copy.56
  82.9 1.6 slice.63
  87.7 1.8 copy.56
  89.6 1.6 slice.63
  94.4 1.8 copy.56
  96.2 1.6 slice.63
  101.0 1.8 copy.56
  102.8 1.6 slice.63
  107.6 1.8 copy.56
  109.5 1.6 slice.63
  114.3 1.8 copy.56
  116.1 1.6 slice.63
  120.9 1.8 copy.56
  122.7 1.6 slice.63
  127.5 1.8 copy.56
  129.4 1.6 slice.63
  134.2 1.8 copy.56
  136.0 1.6 slice.63
  139.7 3.1 fusion.20
  145.1 1.6 fusion.61
  146.7 57.7 %while.22 = (s32[]{:T(128)}, f32[64,2,6144]{2,0,1:T(8,128)}, bf16[9,16,64]{2,1,0:T(8,128)(2,1)}, bf16[16,12288]{1,0:T(8,128)(2,1)S(1)}, f32[9,6144]{1,0:T(8,128)}, /*index=5*/f32[9,6144]{1,0:T(8,128)}, s32[]{:T(128)}, s32[]{:T(128)}) while((s32[]{:T(128)}, f32[64,2,6144]{2,0,1:T(8,128)}, bf16[9,16,64]{2,1,0:T(8,128)(2,1)}, ...), condition=%wide.region_6.7_spmd.clone, body=%wide.region_5.6_spmd.clone.sunk | while | flops 29884416 | bytes 19419748 | solution.py:121
  147.8 1.3 fusion.82
  149.5 2.0 maximum_add_fusion.2
  154.2 3.9 maximum_add_fusion.2
  159.2 1.3 fusion.82
  160.9 3.9 maximum_add_fusion.2
  167.5 3.9 maximum_add_fusion.2
  172.4 1.3 fusion.82
  174.1 3.9 maximum_add_fusion.2
  179.0 1.3 fusion.82
  180.7 3.9 maximum_add_fusion.2
  187.4 3.9 maximum_add_fusion.2
  194.0 3.9 maximum_add_fusion.2
  198.9 1.3 fusion.82
  200.6 3.9 maximum_add_fusion.2
  204.5 3.3 convert_element_type.105
  207.8 2.3 convolution_convert_fusion
  210.2 1.3 dynamic-slice
  212.5 135.4 %all-reduce.9.cloned.1.call-done = (bf16[64,6144]{1,0:T(8,128)(2,1)}, bf16[64,2,6144]{2,0,1:T(8,128)(2,1)}) async-done(((bf16[64,6144]{1,0:T(8,128)(2,1)}, bf16[64,2,6144]{2,0,1:T(8,128)(2,1)}), (bf16[64,6144]{1,0:T(8,128)(2,1)}, bf16[64,2,6144]{2,0,1:T(8,128)(2,1)})) %all-reduce.9.cloned.1.call-update) | async-done | bytes 2359312
  350.9 1.3 dynamic-slice.4
  352.2 134.0 %all-reduce.7.cloned.1.call-done = bf16[16,2,3,6,128]{4,1,3,2,0:T(2,128)(2,1)} async-done(((bf16[16,2,3,6,128]{4,1,3,2,0:T(2,128)(2,1)}), bf16[16,2,3,6,128]{4,1,3,2,0:T(2,128)(2,1)}) %all-reduce.7.cloned.1.call-update) | async-done | bytes 147472
  486.2 1.4 fusion.52
  (114 shorter events, 56.8 us)
Async XLA Ops:
  7.2 66.7 %all-gather.2.cloned.1.call-start = ((), (), s32[]{:S(2)}) async-start(), calls=%async_computation | async-start | bytes 1622016 | tf_op jit(solution)/shard_map/all_gather | solution.py:82
  7.9 340.0 %all-reduce.9.cloned.1.call-start = ((), (), s32[]{:S(2)}) async-start(), calls=%async_computation.2 | async-start | bytes 4718592
  9.2 2.8 copy-start
  9.2 2.7 copy-start.4
  84.6 1.0 copy-start.2
  91.2 1.0 copy-start.2
  97.8 1.0 copy-start.2
  104.5 1.0 copy-start.2
  111.1 1.0 copy-start.2
  117.7 1.0 copy-start.2
  124.4 1.0 copy-start.2
  131.0 1.0 copy-start.2
  137.6 1.0 copy-start.2
  139.7 3.1 copy-start.6
  204.5 3.3 copy-start.3
  204.5 3.3 copy-start.1
  207.8 4.4 copy-start.5
  207.8 4.4 copy-start.7
  210.1 276.1 %all-reduce.7.cloned.1.call-start = ((), (), s32[]{:S(2)}) async-start(), calls=%async_computation.1 | async-start | bytes 294912
Sparse Core Ops, SparseCore 0:
  11.1 62.6 all-gather.1
  210.3 137.5 all-reduce.8
  351.1 135.1 all-reduce.6
where the time goes:
time: 497 us; the launch traced here: 495 us
  waiting for transfers between devices  329 us (66%)
  other arithmetic  63.9 us (13%)
  local copies, waits for them, and re-layouts  58.4 us (12%)
  matrix products  28.5 us (6%)
  between operations  14.6 us (3%)
    unnamed x5, waiting for transfers between devices  270 us
    all_gather x1, waiting for transfers between devices, body(): lax.all_gather(projections, 'dev', axis=0, tiled=True).astype(jnp.float32)  59.3 us
    add x9, other arithmetic, add_shift(): return (running + turned, None)  32.9 us
    dynamic_slice x18, local copies, waits for them, and re-layouts, body(): scored = lax.map(one_shift, (cosines, sine_table))  19 us
    another operation x9, local copies, waits for them, and re-layouts  16.4 us
    slice x9, local copies, waits for them, and re-layouts, one_shift(): values[:, 1] * sin_row[None, :]  14.6 us
    dot_general x9, matrix products, add_shift(): lax.dot_general(weights_now, ctf_image, contract_rows, preferred_element_...  11.4 us
    dot_general x9, matrix products, one_shift(): lax.dot_general(weighted, rotated, contract_last, preferred_element_type=...  10.1 us
  transfers between devices with their start and end apart: 3, of which 3 were waited for; matrix products, arithmetic and copies ran while one was open for 2% of the time, Pallas kernels for 0%

commit v1 on v0

--- a/solution.py
+++ b/solution.py
@@ -79,7 +79,9 @@
     ctf_image = (
         (ctf_rows[:, None, :] * particles).astype(jnp.bfloat16).reshape(part_dev, 2 * pixels)
     )
-    values = lax.all_gather(projections, "dev", axis=0, tiled=True).astype(jnp.float32)
+    values = jnp.concatenate(
+        lax.all_to_all(jnp.stack([projections] * lax.axis_size("dev")), "dev", 0, 0), axis=0
+    ).astype(jnp.float32)
     pix_power = values[:, 0] * values[:, 0] + values[:, 1] * values[:, 1]
     bin_power = lax.dot_general(noisy_square, pix_power, contract_last, precision=exact)
     quad_term = jnp.dot(onehot, bin_power, precision=exact)

time: 497 us -> 466 us (0.938)
  waiting for transfers between devices: 329 us -> 285 us
  starting transfers between devices: 0.12 us -> 10.4 us
    all_gather x1 -> x0, waiting for transfers between devices: 59.3 us -> none  [body(): lax.all_gather(projections, 'dev', axis=0, tiled=True).astype(jnp.float32)]
    all_to_all x0 -> x1, waiting for transfers between devices: none -> 16.7 us  [body(): lax.all_to_all(jnp.stack([projections] * lax.axis_size('dev')), 'dev', 0, 0)]
    all_to_all x0 -> x1, starting transfers between devices: none -> 10.3 us  [body(): lax.all_to_all(jnp.stack([projections] * lax.axis_size('dev')), 'dev', 0, 0)]
    another operation x9 -> x10, local copies, waits for them, and re-layouts: 16.4 us -> 19.8 us
    unnamed x5 -> x4, waiting for transfers between devices: 270 us -> 269 us
where the time goes in v1:
time: 466 us; the launch traced here: 464 us
  waiting for transfers between devices  285 us (61%)
  other arithmetic  62.9 us (13%)
  local copies, waits for them, and re-layouts  62.5 us (13%)
  matrix products  27.5 us (6%)
  between operations  14.9 us (3%)
  starting transfers between devices  10.4 us (2%)
    unnamed x4, waiting for transfers between devices  269 us
    add x9, other arithmetic, add_shift(): return (running + turned, None)  32.8 us
    dynamic_slice x18, local copies, waits for them, and re-layouts, body(): scored = lax.map(one_shift, (cosines, sine_table))  19 us
    all_to_all x1, waiting for transfers between devices, body(): lax.all_to_all(jnp.stack([projections] * lax.axis_size('dev')), 'dev', 0, 0)  16.7 us
    another operation x9, local copies, waits for them, and re-layouts  16.4 us
    slice x9, local copies, waits for them, and re-layouts, one_shift(): values[:, 1] * sin_row[None, :]  14.6 us
    dot_general x9, matrix products, add_shift(): lax.dot_general(weights_now, ctf_image, contract_rows, preferred_element_...  11.4 us
    all_to_all x1, starting transfers between devices, body(): lax.all_to_all(jnp.stack([projections] * lax.axis_size('dev')), 'dev', 0, 0)  10.3 us
  transfers between devices with their start and end apart: 3, of which 3 were waited for; matrix products, arithmetic and copies ran while one was open for 2% of the time, Pallas kernels for 0%

profile of v1, /device:TPU:2, one launch (start us, length us, event | category | flops | bytes accessed | tf_op | source)
XLA Modules:
  0.0 464.0 jit_solution(4436556927493014938)
XLA Ops:
  7.2 3.4 stack.8
  10.6 10.3 %all-to-all-start = ((bf16[32,2,2,6144]{3,2,1,0:T(2,128)(2,1)}), bf16[32,2,2,6144]{3,2,1,0:T(2,128)(2,1)}, u32[]{:S(2)}, u32[]{:S(2)}) async-start(bf16[32,2,2,6144]{3,2,1,0:T(2,128)(2,1)} %stack.8), calls=%async_computation | async-start | bytes 3145728 | tf_op jit(solution)/shard_map/all_to_all | solution.py:83
  23.9 2.5 fusion.30
  26.4 16.7 %all-to-all-done = bf16[32,2,2,6144]{3,2,1,0:T(2,128)(2,1)} async-done(((bf16[32,2,2,6144]{3,2,1,0:T(2,128)(2,1)}), bf16[32,2,2,6144]{3,2,1,0:T(2,128)(2,1)}, u32[]{:S(2)}, u32[]{:S(2)}) %all-to-all-start) | async-done | bytes 1572896 | tf_op jit(solution)/shard_map/all_to_all | solution.py:83
  43.1 3.2 bitcast_convert_fusion
  46.3 3.0 fusion.19
  49.3 59.7 %while.21 = (s32[]{:T(128)}, f32[9,16,64]{2,1,0:T(8,128)}, f32[64,2,6144]{2,1,0:T(2,128)S(1)}, f32[9,6144]{1,0:T(8,128)}, f32[9,6144]{1,0:T(8,128)}, /*index=5*/bf16[16,12288]{1,0:T(8,128)(2,1)}, s32[]{:T(128)}) while((s32[]{:T(128)}, f32[9,16,64]{2,1,0:T(8,128)}, f32[64,2,6144]{2,1,0:T(2,128)S(1)}, f32[9,6144]{1,0:T(8,128)}, ...), condition=%wide.region_2.3_spmd, body=%wide.region_1.2_spmd.sunk | while | flops 31457280 | bytes 17850988 | solution.py:96
  50.4 1.8 copy.56
  52.2 1.6 slice.63
  57.0 1.8 copy.56
  58.9 1.6 slice.63
  63.7 1.8 copy.56
  65.5 1.6 slice.63
  70.3 1.8 copy.56
  72.1 1.6 slice.63
  76.9 1.8 copy.56
  78.8 1.6 slice.63
  83.6 1.8 copy.56
  85.4 1.6 slice.63
  90.2 1.8 copy.56
  92.0 1.6 slice.63
  96.8 1.8 copy.56
  98.7 1.6 slice.63
  103.5 1.8 copy.56
  105.3 1.6 slice.63
  109.0 3.1 fusion.20
  114.4 1.6 fusion.61
  116.0 57.6 %while.22 = (s32[]{:T(128)}, f32[64,2,6144]{2,0,1:T(8,128)}, bf16[9,16,64]{2,1,0:T(8,128)(2,1)}, bf16[16,12288]{1,0:T(8,128)(2,1)S(1)}, f32[9,6144]{1,0:T(8,128)}, /*index=5*/f32[9,6144]{1,0:T(8,128)}, s32[]{:T(128)}, s32[]{:T(128)}) while((s32[]{:T(128)}, f32[64,2,6144]{2,0,1:T(8,128)}, bf16[9,16,64]{2,1,0:T(8,128)(2,1)}, ...), condition=%wide.region_6.7_spmd.clone, body=%wide.region_5.6_spmd.clone.sunk | while | flops 29884416 | bytes 19419748 | solution.py:123
  117.1 1.3 fusion.82
  118.8 2.0 maximum_add_fusion.2
  121.8 1.3 fusion.82
  123.5 3.9 maximum_add_fusion.2
  128.4 1.3 fusion.82
  130.1 3.9 maximum_add_fusion.2
  136.8 3.9 maximum_add_fusion.2
  143.4 3.9 maximum_add_fusion.2
  150.0 3.9 maximum_add_fusion.2
  156.6 3.9 maximum_add_fusion.2
  161.5 1.3 fusion.82
  163.2 3.9 maximum_add_fusion.2
  169.8 3.9 maximum_add_fusion.2
  173.7 3.3 convert_element_type.109
  177.0 2.3 convolution_convert_fusion
  179.4 1.3 dynamic-slice
  181.6 134.6 %all-reduce.9.cloned.1.call-done = (bf16[64,6144]{1,0:T(8,128)(2,1)}, bf16[64,2,6144]{2,0,1:T(8,128)(2,1)}) async-done(((bf16[64,6144]{1,0:T(8,128)(2,1)}, bf16[64,2,6144]{2,0,1:T(8,128)(2,1)}), (bf16[64,6144]{1,0:T(8,128)(2,1)}, bf16[64,2,6144]{2,0,1:T(8,128)(2,1)})) %all-reduce.9.cloned.1.call-update) | async-done | bytes 2359312
  319.3 1.3 dynamic-slice.4
  320.6 134.0 %all-reduce.7.cloned.1.call-done = bf16[16,2,3,6,128]{4,1,3,2,0:T(2,128)(2,1)} async-done(((bf16[16,2,3,6,128]{4,1,3,2,0:T(2,128)(2,1)}), bf16[16,2,3,6,128]{4,1,3,2,0:T(2,128)(2,1)}) %all-reduce.7.cloned.1.call-update) | async-done | bytes 147472
  454.6 1.4 fusion.52
  (120 shorter events, 57.8 us)
Async XLA Ops:
  10.5 10.4 %copy-start.2 = (bf16[16,6144]{1,0:T(8,128)(2,1)S(1)}, bf16[16,6144]{1,0:T(8,128)(2,1)}, u32[]{:S(2)}) copy-start(bf16[16,6144]{1,0:T(8,128)(2,1)} %param.16) | copy-start | bytes 589828
  10.5 10.4 %copy-start.6 = (f32[6144]{0:T(1024)S(1)}, f32[6144]{0:T(1024)}, u32[]{:S(2)}) copy-start(f32[6144]{0:T(1024)} %param.17) | copy-start | bytes 73732
  10.5 10.4 %copy-start.9 = (s32[16]{0:T(128)S(1)}, s32[16]{0:T(128)}, u32[]{:S(2)}) copy-start(s32[16]{0:T(128)} %param.13) | copy-start | bytes 196
  10.5 11.5 %copy-start.4 = (bf16[16,2,6144]{2,1,0:T(2,128)(2,1)S(1)}, bf16[16,2,6144]{2,1,0:T(2,128)(2,1)}, u32[]{:S(2)}) copy-start(bf16[16,2,6144]{2,1,0:T(2,128)(2,1)} %param.12) | copy-start | bytes 1179652
  10.6 32.6 %all-to-all-start = ((bf16[32,2,2,6144]{3,2,1,0:T(2,128)(2,1)}), bf16[32,2,2,6144]{3,2,1,0:T(2,128)(2,1)}, u32[]{:S(2)}, u32[]{:S(2)}) async-start(bf16[32,2,2,6144]{3,2,1,0:T(2,128)(2,1)} %stack.8), calls=%async_computation | async-start | bytes 3145728 | tf_op jit(solution)/shard_map/all_to_all | solution.py:83
  20.9 295.3 %all-reduce.9.cloned.1.call-start = ((), (), s32[]{:S(2)}) async-start(), calls=%async_computation.2 | async-start | bytes 4718592
  21.3 0.8 copy-start
  21.3 2.3 copy-start.7
  53.9 1.0 copy-start.3
  60.5 1.0 copy-start.3
  67.1 1.0 copy-start.3
  73.8 1.0 copy-start.3
  80.4 1.0 copy-start.3
  87.0 1.0 copy-start.3
  93.7 1.0 copy-start.3
  100.3 1.0 copy-start.3
  106.9 1.0 copy-start.3
  173.7 3.3 copy-start.5
  173.7 3.3 copy-start.1
  177.0 4.4 copy-start.8
  177.0 4.3 copy-start.10
  179.3 275.2 %all-reduce.7.cloned.1.call-start = ((), (), s32[]{:S(2)}) async-start(), calls=%async_computation.1 | async-start | bytes 294912
Sparse Core Ops, SparseCore 0:
  179.5 136.7 all-reduce.8
  319.5 135.0 all-reduce.6
